TPU v7x, 128 devices: a whole 4x4x4 slice. The times are simulated.
128 devices in a mesh: heads: 8 (over z, core), width: 4 (over y), sae: 4 (over x).
Axes of the slice: x: 4, y: 4, z: 4, core: 2. Of those that a mesh axis runs over, the one named last changes fastest.
Arguments:
- x_in: bfloat16 [512, 4608], P(None, 'width'), may hold values from -64 to 64
- doc_lengths: int32 [4], replicated, may hold values from 1 to 256, 512 in all
- attn_gain: float32 [4608], P('width'), may hold values from 0.25 to 1.75
- w_query: bfloat16 [4608, 4096], P('width', 'heads'), may hold values from -0.09375 to 0.09375
- w_key: bfloat16 [4608, 2048], P('width', 'heads'), may hold values from -0.09375 to 0.09375
- w_value: bfloat16 [4608, 2048], P('width', 'heads'), may hold values from -0.09375 to 0.09375
- w_out: bfloat16 [4096, 4608], P('heads', 'width'), may hold values from -0.09375 to 0.09375
- post_gain: float32 [4608], replicated, may hold values from 0.25 to 1.75
- enc_weight: bfloat16 [4608, 65536], P(None, ('heads', 'width', 'sae')), may hold values from -0.09375 to 0.09375
- enc_bias: float32 [65536], P(('heads', 'width', 'sae')), may hold values from -1.5 to 0.5
- dec_weight: bfloat16 [65536, 4608], P(('heads', 'width', 'sae')), may hold values from -1 to 1
- dec_bias: float32 [4608], replicated, may hold values from -5 to 5
Outputs:
- grad_enc: bfloat16 [4608, 65536], P(None, ('heads', 'width', 'sae'))
- grad_dec: bfloat16 [65536, 4608], P(('heads', 'width', 'sae'))
- total_loss: float32 [], replicated
Inputs may be any that keep to these rules, and one draw needn't show every extreme that they name: `doc_lengths`: lengths of the 4 documents packed in order; they sum to 512.
All inputs are finite; a program needn't handle non-finite values.
Results may differ from a plain program's by a relative error of at most 0.02.
Values may be sent and summed in bfloat16 or wider, within the bound.
A program may use at most 128 MiB of HBM per device.

v0:
```python
import jax
import jax.numpy as jnp
from jax import lax
from jax.sharding import PartitionSpec as P

D = 4608
HEADS = 32
HEAD_DIM = 128
norm_eps = 1e-06
soft_cap = 50.0
rope_base = 10000.0
l1_weight = 3.0


def rotary(values, position):
    half_dim = values.shape[-1] // 2
    frequency = rope_base ** (-2.0 * jnp.arange(half_dim, dtype=jnp.float32) / values.shape[-1])
    angles = position.astype(jnp.float32)[:, None] * frequency[None, :]
    cosine_table = jnp.cos(angles)[:, None, :]
    sine_table = jnp.sin(angles)[:, None, :]
    first_half = values[..., :half_dim]
    second_half = values[..., half_dim:]
    return jnp.concatenate(
        [
            first_half * cosine_table - second_half * sine_table,
            second_half * cosine_table + first_half * sine_table,
        ],
        axis=-1,
    )


def attend_rows(query_rows, key_rows, value_rows, allowed_rows, scale):
    scores = (
        jnp.einsum("tkgd,skd->kgts", query_rows, key_rows, preferred_element_type=jnp.float32)
        * scale
    )
    capped = soft_cap * jnp.tanh(scores / soft_cap)
    weights = jnp.where(allowed_rows[None, None], jnp.exp(capped), 0.0)
    totals = jnp.sum(weights, axis=-1, keepdims=True)
    probs_bf = (weights / totals).astype(jnp.bfloat16)
    return jnp.einsum(
        "kgts,skd->tkgd", probs_bf, value_rows, preferred_element_type=jnp.float32
    ).astype(jnp.bfloat16)


def per_device(
    x_in,
    doc_lengths,
    attn_gain,
    w_query,
    w_key,
    w_value,
    w_out,
    post_gain,
    enc_weight,
    enc_bias,
    dec_weight,
    dec_bias,
):
    tokens = x_in.shape[0]
    query_heads = w_query.shape[1] // HEAD_DIM
    value_heads = w_key.shape[1] // HEAD_DIM
    boundary = jnp.cumsum(doc_lengths)
    position = jnp.arange(tokens, dtype=jnp.int32)
    segment = jnp.sum((boundary[None, :] <= position[:, None]).astype(jnp.int32), axis=1)
    allowed = (segment[:, None] == segment[None, :]) & (position[None, :] <= position[:, None])
    x_float = x_in.astype(jnp.float32)
    scaled = (x_float * attn_gain).astype(jnp.bfloat16)
    query_part = jnp.dot(scaled, w_query, preferred_element_type=jnp.float32)
    key_part = jnp.dot(scaled, w_key, preferred_element_type=jnp.float32)
    value_part = jnp.dot(scaled, w_value, preferred_element_type=jnp.float32)
    square_part = jnp.sum(x_float * x_float, axis=1)
    query_raw, key_raw, value_raw, square_sums = lax.psum(
        (query_part, key_part, value_part, square_part), "width"
    )
    inverse_rms = lax.rsqrt(square_sums / D + norm_eps)
    query = rotary(
        (query_raw * inverse_rms[:, None]).reshape(tokens, query_heads, HEAD_DIM), position
    ).astype(jnp.bfloat16)
    key_rows = rotary(
        (key_raw * inverse_rms[:, None]).reshape(tokens, value_heads, HEAD_DIM), position
    ).astype(jnp.bfloat16)
    value_rows = (
        (value_raw * inverse_rms[:, None])
        .reshape(tokens, value_heads, HEAD_DIM)
        .astype(jnp.bfloat16)
    )
    query4 = query.reshape(tokens, value_heads, query_heads // value_heads, HEAD_DIM)
    pieces_out = attend_rows(query4, key_rows, value_rows, allowed, (D // HEADS) ** (-0.5))
    mixed = pieces_out.reshape(tokens, query_heads * HEAD_DIM)
    proj_part = jnp.dot(mixed, w_out, preferred_element_type=jnp.float32)
    attn_sum = lax.psum(proj_part, "heads")
    attn_local = attn_sum.astype(jnp.bfloat16)
    attn_proj, x_full = (
        lax.all_gather(attn_local, "width", axis=1, tiled=True),
        lax.all_gather(x_in, "width", axis=1, tiled=True),
    )
    proj_float = attn_proj.astype(jnp.float32)
    inverse_post = lax.rsqrt(jnp.sum(proj_float * proj_float, axis=1) / D + norm_eps)
    resid = (x_full.astype(jnp.float32) + proj_float * inverse_post[:, None] * post_gain).astype(
        jnp.bfloat16
    )
    centered = (resid.astype(jnp.float32) - dec_bias).astype(jnp.bfloat16)
    pre_acts = jnp.dot(centered, enc_weight, preferred_element_type=jnp.float32) + enc_bias
    latent_acts = jnp.maximum(pre_acts, 0.0).astype(jnp.bfloat16)
    row_norms = jnp.sqrt(jnp.sum(jnp.square(dec_weight.astype(jnp.float32)), axis=1) + norm_eps)
    act_sums = jnp.sum(latent_acts.astype(jnp.float32), axis=0)
    penalty_part = jnp.sum(act_sums * row_norms)
    recon_part = jnp.dot(latent_acts, dec_weight, preferred_element_type=jnp.float32)
    recon = lax.psum(recon_part, ("heads", "width", "sae")) + dec_bias
    error = recon - resid.astype(jnp.float32)
    squares_total = jnp.sum(error * error)
    penalty_total = lax.psum(penalty_part, ("heads", "width", "sae"))
    grad_recon = (2.0 / tokens * error).astype(jnp.bfloat16)
    total_loss = (squares_total + l1_weight * penalty_total) / (tokens * D)
    upstream = lax.dot_general(
        grad_recon, dec_weight, (((1,), (1,)), ((), ())), preferred_element_type=jnp.float32
    )
    grad_pre = jnp.where(pre_acts > 0, upstream + l1_weight * row_norms / tokens, 0.0).astype(
        jnp.bfloat16
    )
    grad_enc = lax.dot_general(
        centered, grad_pre, (((0,), (0,)), ((), ())), preferred_element_type=jnp.float32
    ).astype(jnp.bfloat16)
    decoder_term = lax.dot_general(
        latent_acts, grad_recon, (((0,), (0,)), ((), ())), preferred_element_type=jnp.float32
    )
    grad_dec = (
        decoder_term
        + l1_weight
        / tokens
        * act_sums[:, None]
        * dec_weight.astype(jnp.float32)
        / row_norms[:, None]
    ).astype(jnp.bfloat16)
    return (grad_enc, grad_dec, total_loss)


def solution(mesh):
    placed = (
        P(None, "width"),
        P(),
        P("width"),
        P("width", "heads"),
        P("width", "heads"),
        P("width", "heads"),
        P("heads", "width"),
        P(),
        P(None, ("heads", "width", "sae")),
        P(("heads", "width", "sae")),
        P(("heads", "width", "sae"), None),
        P(),
    )
    return jax.shard_map(
        per_device,
        mesh=mesh,
        in_specs=placed,
        out_specs=(P(None, ("heads", "width", "sae")), P(("heads", "width", "sae"), None), P()),
        check_vma=False,
    )
```

profile of v0, /device:TPU:1, one launch (start us, length us, event | category | flops | bytes accessed | tf_op | source)
XLA Modules:
  0.0 471.6 jit_solution(9375944868353371698)
XLA Ops:
  7.3 3.6 fusion.23
  10.9 2.7 fusion.25
  15.5 9.5 %psum.50 = f32[512]{0:T(512)S(1)} all-reduce(f32[512]{0:T(512)S(1)} %fusion.14), channel_id=1, replica_groups=mesh['heads'=8,'width'=4,'sae'=4] {'width'}, use_global_device_ids=true, to_apply=%region_2.3 | all-reduce | flops 512 | bytes 4096 | tf_op jit(solution)/shard_map/psum | solution.py:73
  26.1 1.7 multiply_cosine_fusion
  27.8 49.0 %all-reduce.7.cloned.1.call-done = (f32[512,256]{1,0:T(8,128)}, f32[512,512]{1,0:T(8,128)}, f32[512,256]{1,0:T(8,128)}) async-done(((f32[512,256]{1,0:T(8,128)}, f32[512,512]{1,0:T(8,128)}, f32[512,256]{1,0:T(8,128)}), (f32[512,256]{1,0:T(8,128)}, f32[512,512]{1,0:T(8,128)}, f32[512,256]{1,0:T(8,128)})) %all-reduce.7.cloned.1.call-update) | async-done | bytes 2097168 | tf_op jit(solution)/shard_map/psum | solution.py:73
  76.9 2.1 broadcast_multiply_fusion.1
  79.2 1.5 fusion.40
  82.5 1.8 subtract_convert_fusion
  85.9 2.9 fusion.12
  88.8 1.6 fusion.21
  91.3 52.5 %all-reduce.8 = bf16[512,1152]{1,0:T(8,128)(2,1)} all-reduce(f32[512,1152]{1,0:T(8,128)S(1)} %fusion.41), channel_id=1, replica_groups=mesh['heads'=8,'width'=4,'sae'=4] {'heads'}, use_global_device_ids=true, to_apply=%region_8.9 | all-reduce | flops 589824 | bytes 3538944 | tf_op jit(solution)/shard_map/psum | solution.py:92
  144.8 51.8 %all-gather.5.cloned.1.call-done = bf16[512,4608]{1,0:T(8,128)(2,1)} async-done(((bf16[512,1152]{1,0:T(8,128)(2,1)}), bf16[512,4608]{1,0:T(8,128)(2,1)}) %all-gather.5.cloned.1.call-update) | async-done | bytes 4718608 | tf_op jit(solution)/shard_map/all_gather | solution.py:95
  196.6 3.3 fusion
  200.0 51.3 %all-gather.3.cloned.1.call-done = bf16[512,4608]{1,0:T(8,128)(2,1)} async-done(((bf16[512,1152]{1,0:T(8,128)(2,1)}), bf16[512,4608]{1,0:T(8,128)(2,1)}) %all-gather.3.cloned.1.call-update) | async-done | bytes 4718608 | tf_op jit(solution)/shard_map/all_gather | solution.py:96
  251.3 5.9 %fusion.3 = bf16[512,4608]{1,0:T(8,128)(2,1)S(1)} fusion(bf16[512,4608]{1,0:T(8,128)(2,1)} %all-gather.5.cloned.1.call-done, bf16[512,4608]{1,0:T(8,128)(2,1)} %all-gather.3.cloned.1.call-done, f32[4608]{0:T(1024)S(1)} %copy-done.8, f32[512]{0:T(512)S(1)} %add_rsqrt_fusion), kind=kLoop, calls=%fused_computation.9 | loop fusion | flops 14155776 | bytes 14176256 | tf_op jit(solution)/shard_map/convert_element_type | solution.py:100
  257.3 6.4 %convert_reduce_fusion = (f32[512]{0:T(512)S(1)}, f32[512,512]{1,0:T(8,128)S(1)}) fusion(f32[512]{0:T(512)S(1)} %copy-done.12, bf16[4608,512]{1,0:T(8,128)(2,1)} %param.20, bf16[512,4608]{1,0:T(8,128)(2,1)S(1)} %fusion.3, f32[4608]{0:T(1024)S(1)} %copy-done.9), kind=kOutput, calls=%fused_computation.32 | convolution fusion | flops 2424045056 | bytes 10508288 | tf_op jit(solution)/shard_map/dot_general | solution.py:104
  263.7 5.1 %fusion.39 = f32[512,4608]{1,0:T(8,128)} fusion(bf16[512,4608]{1,0:T(8,128)(2,1)S(1)} %bitcast.41, f32[512,512]{1,0:T(8,128)S(1)} %get-tuple-element.25), kind=kOutput, calls=%fused_computation.69 | convolution fusion | flops 2416443392 | bytes 15204352 | tf_op jit(solution)/shard_map/dot_general | solution.py:109
  268.8 3.3 fusion.5
  272.8 65.8 %psum.55 = f32[]{:T(128)} all-reduce(f32[]{:T(128)} %get-tuple-element.16), channel_id=1, replica_groups=mesh['heads'=8,'width'=4,'sae'=4] {'heads','width','sae'}, use_global_device_ids=true, to_apply=%region_15.16 | all-reduce | flops 1 | bytes 8 | tf_op jit(solution)/shard_map/psum | solution.py:113
  339.2 94.4 %all-reduce.5.cloned.1.call-done = f32[512,4608]{1,0:T(8,128)} async-done(((f32[512,4608]{1,0:T(8,128)}), f32[512,4608]{1,0:T(8,128)}) %all-reduce.5.cloned.1.call-update) | async-done | bytes 9437200 | tf_op jit(solution)/shard_map/psum | solution.py:110
  433.6 8.4 %multiply_reduce_fusion = (f32[]{:T(128)}, bf16[512,4608]{1,0:T(8,128)(2,1)S(1)}) fusion(bf16[512,4608]{1,0:T(8,128)(2,1)} %copy-done.2, f32[512,4608]{1,0:T(8,128)} %all-reduce.5.cloned.1.call-done, f32[4608]{0:T(1024)S(1)} %copy-done.9), kind=kLoop, calls=%fused_computation.15 | loop fusion | flops 16515071 | bytes 18892804 | tf_op jit(solution)/shard_map/reduce_sum | solution.py:112
  442.0 6.7 %fusion.20 = bf16[512,512]{1,0:T(8,128)(2,1)S(1)} fusion(bf16[512,4608]{1,0:T(8,128)(2,1)S(1)} %get-tuple-element.7, bf16[512,4608]{1,0:T(8,128)(2,1)} %param.22, f32[512,512]{1,0:T(8,128)S(1)} %get-tuple-element.25, f32[512]{0:T(512)S(1)} %get-tuple-element.17), kind=kOutput, calls=%fused_computation.30 | convolution fusion | flops 2416967680 | bytes 11012096 | tf_op jit(solution)/shard_map/dot_general | solution.py:116
  448.7 6.8 %convolution_convert_fusion = bf16[4608,512]{1,0:T(8,128)(2,1)} fusion(bf16[512,512]{1,0:T(8,128)(2,1)S(1)} %fusion.20, bf16[512,4608]{1,0:T(8,128)(2,1)} %copy-done.2, f32[4608]{0:T(1024)S(1)} %copy-done.9), kind=kOutput, calls=%fused_computation.17 | convolution fusion | flops 2425356288 | bytes 9979904 | tf_op jit(solution)/shard_map/dot_general | solution.py:122
  456.1 7.8 %fusion.8 = bf16[512,4608]{1,0:T(8,128)(2,1)} fusion(bf16[512,4608]{1,0:T(8,128)(2,1)} %param.22, bf16[512,4608]{1,0:T(8,128)(2,1)} %copy-done.4, f32[512]{0:T(512)S(1)} %get-tuple-element.18, f32[512]{0:T(512)S(1)} %get-tuple-element.19, f32[512,512]{1,0:T(8,128)S(1)} %get-tuple-element.25), kind=kOutput, calls=%fused_computation.14 | convolution fusion | flops 2428239872 | bytes 15208448 | tf_op jit(solution)/shard_map/dot_general | solution.py:125
  (59 shorter events, 9.1 us)
Async XLA Ops:
  7.2 83.3 %copy-start = (bf16[512,1152]{1,0:T(8,128)(2,1)S(1)}, bf16[512,1152]{1,0:T(8,128)(2,1)}, u32[]{:S(2)}) copy-start(bf16[512,1152]{1,0:T(8,128)(2,1)} %param.18) | copy-start | bytes 3538948
  7.2 6.5 %copy-start.3 = (bf16[512,1152]{1,0:T(8,128)(2,1)S(1)}, bf16[512,1152]{1,0:T(8,128)(2,1)}, u32[]{:S(2)}) copy-start(bf16[512,1152]{1,0:T(8,128)(2,1)} %param.12) | copy-start | bytes 3538948
  7.2 6.4 %copy-start.11 = (f32[1152]{0:T(1024)S(1)}, f32[1152]{0:T(1024)}, u32[]{:S(2)}) copy-start(f32[1152]{0:T(1024)} %param.14) | copy-start | bytes 13828
  7.2 6.4 %copy-start.10 = (bf16[1152,256]{1,0:T(8,128)(2,1)S(1)}, bf16[1152,256]{1,0:T(8,128)(2,1)}, u32[]{:S(2)}) copy-start(bf16[1152,256]{1,0:T(8,128)(2,1)} %param.17) | copy-start | bytes 1769476
  7.2 7.8 %copy-start.13 = (s32[4]{0:T(128)S(1)}, s32[4]{0:T(128)}, u32[]{:S(2)}) copy-start(s32[4]{0:T(128)} %param.13) | copy-start | bytes 52
  7.2 69.6 %all-reduce.7.cloned.1.call-start = ((), (), s32[]{:S(2)}) async-start(), calls=%async_computation.3 | async-start | bytes 4194304 | tf_op jit(solution)/shard_map/psum | solution.py:73
  15.0 181.6 %all-gather.5.cloned.1.call-start = ((), (), s32[]{:S(2)}) async-start(), calls=%async_computation.1 | async-start | bytes 5898240 | tf_op jit(solution)/shard_map/all_gather | solution.py:95
  82.4 2.0 copy-start.6
  82.4 2.1 copy-start.5
  85.9 2.9 copy-start.7
  91.3 160.0 %copy-start.8 = (f32[4608]{0:T(1024)S(1)}, f32[4608]{0:T(1024)}, u32[]{:S(2)}) copy-start(f32[4608]{0:T(1024)} %param.19) | copy-start | bytes 55300
  143.8 107.5 %all-gather.3.cloned.1.call-start = ((), (), s32[]{:S(2)}) async-start(), calls=%async_computation | async-start | bytes 5898240 | tf_op jit(solution)/shard_map/all_gather | solution.py:96
  144.5 289.1 %all-reduce.5.cloned.1.call-start = ((), (), s32[]{:S(2)}) async-start(), calls=%async_computation.2 | async-start | bytes 18874368 | tf_op jit(solution)/shard_map/psum | solution.py:110
  199.9 57.3 %copy-start.9 = (f32[4608]{0:T(1024)S(1)}, f32[4608]{0:T(1024)}, u32[]{:S(2)}) copy-start(f32[4608]{0:T(1024)} %param.23) | copy-start | bytes 55300
  199.9 57.3 %copy-start.12 = (f32[512]{0:T(512)S(1)}, f32[512]{0:T(512)}, u32[]{:S(2)}) copy-start(f32[512]{0:T(512)} %param.21) | copy-start | bytes 6148
  251.3 12.4 %slice-start = ((s8[4718592]{0:T(1024)(128)(4,1)}), s8[4194304]{0:T(1024)(128)(4,1)S(1)}, s32[]{:S(2)}) async-start(s8[4718592]{0:T(1024)(128)(4,1)} %bitcast.40), calls=%async_computation.4 | async-start | bytes 8388608
  257.2 6.4 %copy-start.2 = (bf16[512,4608]{1,0:T(8,128)(2,1)}, bf16[512,4608]{1,0:T(8,128)(2,1)S(1)}, u32[]{:S(2)}) copy-start(bf16[512,4608]{1,0:T(8,128)(2,1)S(1)} %fusion.3) | copy-start | bytes 14155780
  257.2 6.5 %slice-start.1 = ((s8[4718592]{0:T(1024)(128)(4,1)}), s8[524288]{0:T(1024)(128)(4,1)S(1)}, s32[]{:S(2)}) async-start(s8[4718592]{0:T(1024)(128)(4,1)} %bitcast.40), calls=%async_computation.5 | async-start | bytes 1048576
  442.0 6.7 %copy-start.4 = (bf16[512,4608]{1,0:T(8,128)(2,1)}, bf16[512,4608]{1,0:T(8,128)(2,1)S(1)}, u32[]{:S(2)}) copy-start(bf16[512,4608]{1,0:T(8,128)(2,1)S(1)} %get-tuple-element.7) | copy-start | bytes 14155780
  456.1 7.9 %copy-start.1 = (bf16[512,1152]{1,0:T(8,128)(2,1)S(1)}, bf16[512,1152]{1,0:T(8,128)(2,1)}, u32[]{:S(2)}) copy-start(bf16[512,1152]{1,0:T(8,128)(2,1)} %param.18) | copy-start | bytes 3538948
Sparse Core Ops, SparseCore 0:
  15.1 61.7 all-reduce.6
  143.9 52.6 all-gather.4
  198.3 52.9 all-gather.2
  268.9 164.6 all-reduce.4
where the time goes:
time: 472 us
  waiting for transfers between devices  247 us (52%)
  blocking collectives  128 us (27%)
  matrix products  45.7 us (10%)
  other arithmetic  31.4 us (7%)
  between operations  16.5 us (3%)
    psum x1, waiting for transfers between devices, per_device(): recon = lax.psum(recon_part, ('heads', 'width', 'sae')) + dec_bias  94.4 us
    psum x1, blocking collectives, per_device(): penalty_total = lax.psum(penalty_part, ('heads', 'width', 'sae'))  65.8 us
    psum x1, blocking collectives, per_device(): attn_sum = lax.psum(proj_part, 'heads')  52.5 us
    all_gather x1, waiting for transfers between devices, per_device(): lax.all_gather(attn_local, 'width', axis=1, tiled=True)  51.8 us
    all_gather x1, waiting for transfers between devices, per_device(): lax.all_gather(x_in, 'width', axis=1, tiled=True)  51.3 us
    psum x1, waiting for transfers between devices, per_device(): lax.psum((query_part, key_part, value_part, square_part), 'width')  49 us
    psum x1, blocking collectives, per_device(): lax.psum((query_part, key_part, value_part, square_part), 'width')  9.54 us
  transfers between devices with their start and end apart: 4, of which 4 were waited for; matrix products, arithmetic and copies ran while one was open for 2% of the time, Pallas kernels for 0%

commit v1 on v0

--- a/solution.py
+++ b/solution.py
@@ -107,7 +107,7 @@
     act_sums = jnp.sum(latent_acts.astype(jnp.float32), axis=0)
     penalty_part = jnp.sum(act_sums * row_norms)
     recon_part = jnp.dot(latent_acts, dec_weight, preferred_element_type=jnp.float32)
-    recon = lax.psum(recon_part, ("heads", "width", "sae")) + dec_bias
+    recon = jax.lax.psum(jax.lax.psum(recon_part, "heads"), ("width", "sae")) + dec_bias
     error = recon - resid.astype(jnp.float32)
     squares_total = jnp.sum(error * error)
     penalty_total = lax.psum(penalty_part, ("heads", "width", "sae"))

time: 472 us -> 576 us (1.22)
  waiting for transfers between devices: 247 us -> 349 us
    psum x1 -> x2, waiting for transfers between devices: 94.4 us -> 196 us  [the longest x1 114 us: per_device(): jax.lax.psum(recon_part, 'heads')]
  transfers between devices with their start and end apart: 4 -> 5, of which waited for: 4 -> 5; matrix products, arithmetic and copies ran while one was open for 2% -> 2% of each run, Pallas kernels for 0% -> 0%
where the time goes in v1:
time: 576 us; the launch traced here: 575 us
  waiting for transfers between devices  349 us (61%)
  blocking collectives  130 us (23%)
  matrix products  45.7 us (8%)
  other arithmetic  31.4 us (5%)
  between operations  16.5 us (3%)
    psum x1, waiting for transfers between devices, per_device(): jax.lax.psum(recon_part, 'heads')  114 us
    psum x1, waiting for transfers between devices, per_device(): jax.lax.psum(jax.lax.psum(recon_part, 'heads'), ('width', 'sae')) + dec_bias  81.3 us
    psum x1, blocking collectives, per_device(): penalty_total = lax.psum(penalty_part, ('heads', 'width', 'sae'))  68.1 us
    psum x1, blocking collectives, per_device(): attn_sum = lax.psum(proj_part, 'heads')  52.5 us
    all_gather x1, waiting for transfers between devices, per_device(): lax.all_gather(attn_local, 'width', axis=1, tiled=True)  51.8 us
    all_gather x1, waiting for transfers between devices, per_device(): lax.all_gather(x_in, 'width', axis=1, tiled=True)  51.3 us
    psum x1, waiting for transfers between devices, per_device(): lax.psum((query_part, key_part, value_part, square_part), 'width')  49 us
  transfers between devices with their start and end apart: 5, of which 5 were waited for; matrix products, arithmetic and copies ran while one was open for 2% of the time, Pallas kernels for 0%

profile of v1, /device:TPU:1, one launch (start us, length us, event | category | flops | bytes accessed | tf_op | source)
XLA Modules:
  0.0 575.3 jit_solution(15833149714313977171)
XLA Ops:
  7.3 3.6 fusion.23
  10.9 2.7 fusion.25
  15.5 9.5 %psum.57 = f32[512]{0:T(512)S(1)} all-reduce(f32[512]{0:T(512)S(1)} %fusion.14), channel_id=1, replica_groups=mesh['heads'=8,'width'=4,'sae'=4] {'width'}, use_global_device_ids=true, to_apply=%region_2.3 | all-reduce | flops 512 | bytes 4096 | tf_op jit(solution)/shard_map/psum | solution.py:73
  26.1 1.7 multiply_cosine_fusion
  27.8 49.0 %all-reduce.10.cloned.1.call-done = (f32[512,256]{1,0:T(8,128)}, f32[512,512]{1,0:T(8,128)}, f32[512,256]{1,0:T(8,128)}) async-done(((f32[512,256]{1,0:T(8,128)}, f32[512,512]{1,0:T(8,128)}, f32[512,256]{1,0:T(8,128)}), (f32[512,256]{1,0:T(8,128)}, f32[512,512]{1,0:T(8,128)}, f32[512,256]{1,0:T(8,128)})) %all-reduce.10.cloned.1.call-update) | async-done | bytes 2097168 | tf_op jit(solution)/shard_map/psum | solution.py:73
  76.9 2.1 broadcast_multiply_fusion.1
  82.5 1.8 subtract_convert_fusion
  86.0 2.9 fusion.12
  88.9 1.6 fusion.21
  91.3 52.5 %all-reduce.11 = bf16[512,1152]{1,0:T(8,128)(2,1)} all-reduce(f32[512,1152]{1,0:T(8,128)S(1)} %fusion.41), channel_id=1, replica_groups=mesh['heads'=8,'width'=4,'sae'=4] {'heads'}, use_global_device_ids=true, to_apply=%region_8.9 | all-reduce | flops 589824 | bytes 3538944 | tf_op jit(solution)/shard_map/psum | solution.py:92
  144.8 51.8 %all-gather.5.cloned.1.call-done = bf16[512,4608]{1,0:T(8,128)(2,1)} async-done(((bf16[512,1152]{1,0:T(8,128)(2,1)}), bf16[512,4608]{1,0:T(8,128)(2,1)}) %all-gather.5.cloned.1.call-update) | async-done | bytes 4718608 | tf_op jit(solution)/shard_map/all_gather | solution.py:95
  196.6 3.3 fusion
  200.0 51.3 %all-gather.3.cloned.1.call-done = bf16[512,4608]{1,0:T(8,128)(2,1)} async-done(((bf16[512,1152]{1,0:T(8,128)(2,1)}), bf16[512,4608]{1,0:T(8,128)(2,1)}) %all-gather.3.cloned.1.call-update) | async-done | bytes 4718608 | tf_op jit(solution)/shard_map/all_gather | solution.py:96
  251.3 5.9 %fusion.3 = bf16[512,4608]{1,0:T(8,128)(2,1)S(1)} fusion(bf16[512,4608]{1,0:T(8,128)(2,1)} %all-gather.5.cloned.1.call-done, bf16[512,4608]{1,0:T(8,128)(2,1)} %all-gather.3.cloned.1.call-done, f32[4608]{0:T(1024)S(1)} %copy-done.8, f32[512]{0:T(512)S(1)} %add_rsqrt_fusion), kind=kLoop, calls=%fused_computation.9 | loop fusion | flops 14155776 | bytes 14176256 | tf_op jit(solution)/shard_map/convert_element_type | solution.py:100
  257.3 6.4 %convert_reduce_fusion = (f32[512]{0:T(512)S(1)}, f32[512,512]{1,0:T(8,128)S(1)}) fusion(f32[512]{0:T(512)S(1)} %copy-done.12, bf16[4608,512]{1,0:T(8,128)(2,1)} %param.20, bf16[512,4608]{1,0:T(8,128)(2,1)S(1)} %fusion.3, f32[4608]{0:T(1024)S(1)} %copy-done.9), kind=kOutput, calls=%fused_computation.32 | convolution fusion | flops 2424045056 | bytes 10508288 | tf_op jit(solution)/shard_map/dot_general | solution.py:104
  263.7 5.1 fusion.39
  268.9 114.4 %all-reduce.6.cloned.1.call-done = f32[512,4608]{1,0:T(8,128)} async-done(((f32[512,4608]{1,0:T(8,128)}), f32[512,4608]{1,0:T(8,128)}) %all-reduce.6.cloned.1.call-update) | async-done | bytes 9437200 | tf_op jit(solution)/shard_map/psum | solution.py:110
  383.3 3.3 fusion.5
  387.3 68.1 %psum.63 = f32[]{:T(128)} all-reduce(f32[]{:T(128)} %get-tuple-element.16), channel_id=1, replica_groups=mesh['heads'=8,'width'=4,'sae'=4] {'heads','width','sae'}, use_global_device_ids=true, to_apply=%region_16.17 | all-reduce | flops 1 | bytes 8 | tf_op jit(solution)/shard_map/psum | solution.py:113
  456.0 81.3 %all-reduce.8.cloned.1.call-done = f32[512,4608]{1,0:T(8,128)} async-done(((f32[512,4608]{1,0:T(8,128)}), f32[512,4608]{1,0:T(8,128)}) %all-reduce.8.cloned.1.call-update) | async-done | bytes 9437200 | tf_op jit(solution)/shard_map/psum | solution.py:110
  537.3 8.4 %multiply_reduce_fusion = (f32[]{:T(128)}, bf16[512,4608]{1,0:T(8,128)(2,1)S(1)}) fusion(bf16[512,4608]{1,0:T(8,128)(2,1)} %copy-done.2, f32[512,4608]{1,0:T(8,128)} %all-reduce.8.cloned.1.call-done, f32[4608]{0:T(1024)S(1)} %copy-done.9), kind=kLoop, calls=%fused_computation.15 | loop fusion | flops 16515071 | bytes 18892804 | tf_op jit(solution)/shard_map/reduce_sum | solution.py:112
  545.6 6.7 %fusion.20 = bf16[512,512]{1,0:T(8,128)(2,1)S(1)} fusion(bf16[512,4608]{1,0:T(8,128)(2,1)S(1)} %get-tuple-element.7, bf16[512,4608]{1,0:T(8,128)(2,1)} %param.22, f32[512,512]{1,0:T(8,128)S(1)} %get-tuple-element.25, f32[512]{0:T(512)S(1)} %get-tuple-element.17), kind=kOutput, calls=%fused_computation.30 | convolution fusion | flops 2416967680 | bytes 11012096 | tf_op jit(solution)/shard_map/dot_general | solution.py:116
  552.3 6.7 %convolution_convert_fusion = bf16[4608,512]{1,0:T(8,128)(2,1)} fusion(bf16[512,512]{1,0:T(8,128)(2,1)S(1)} %fusion.20, bf16[512,4608]{1,0:T(8,128)(2,1)} %copy-done.2, f32[4608]{0:T(1024)S(1)} %copy-done.9), kind=kOutput, calls=%fused_computation.17 | convolution fusion | flops 2425356288 | bytes 9979904 | tf_op jit(solution)/shard_map/dot_general | solution.py:122
  559.7 7.8 %fusion.8 = bf16[512,4608]{1,0:T(8,128)(2,1)} fusion(bf16[512,4608]{1,0:T(8,128)(2,1)} %param.22, bf16[512,4608]{1,0:T(8,128)(2,1)} %copy-done.4, f32[512]{0:T(512)S(1)} %get-tuple-element.18, f32[512]{0:T(512)S(1)} %get-tuple-element.19, f32[512,512]{1,0:T(8,128)S(1)} %get-tuple-element.25), kind=kOutput, calls=%fused_computation.14 | convolution fusion | flops 2428239872 | bytes 15208448 | tf_op jit(solution)/shard_map/dot_general | solution.py:125
  (62 shorter events, 10.7 us)
Async XLA Ops:
  7.2 83.3 %copy-start = (bf16[512,1152]{1,0:T(8,128)(2,1)S(1)}, bf16[512,1152]{1,0:T(8,128)(2,1)}, u32[]{:S(2)}) copy-start(bf16[512,1152]{1,0:T(8,128)(2,1)} %param.18) | copy-start | bytes 3538948
  7.2 6.5 %copy-start.3 = (bf16[512,1152]{1,0:T(8,128)(2,1)S(1)}, bf16[512,1152]{1,0:T(8,128)(2,1)}, u32[]{:S(2)}) copy-start(bf16[512,1152]{1,0:T(8,128)(2,1)} %param.12) | copy-start | bytes 3538948
  7.2 6.4 %copy-start.11 = (f32[1152]{0:T(1024)S(1)}, f32[1152]{0:T(1024)}, u32[]{:S(2)}) copy-start(f32[1152]{0:T(1024)} %param.14) | copy-start | bytes 13828
  7.2 6.4 %copy-start.10 = (bf16[1152,256]{1,0:T(8,128)(2,1)S(1)}, bf16[1152,256]{1,0:T(8,128)(2,1)}, u32[]{:S(2)}) copy-start(bf16[1152,256]{1,0:T(8,128)(2,1)} %param.17) | copy-start | bytes 1769476
  7.2 7.8 %copy-start.13 = (s32[4]{0:T(128)S(1)}, s32[4]{0:T(128)}, u32[]{:S(2)}) copy-start(s32[4]{0:T(128)} %param.13) | copy-start | bytes 52
  7.2 69.6 %all-reduce.10.cloned.1.call-start = ((), (), s32[]{:S(2)}) async-start(), calls=%async_computation.4 | async-start | bytes 4194304 | tf_op jit(solution)/shard_map/psum | solution.py:73
  15.0 181.6 %all-gather.5.cloned.1.call-start = ((), (), s32[]{:S(2)}) async-start(), calls=%async_computation.1 | async-start | bytes 5898240 | tf_op jit(solution)/shard_map/all_gather | solution.py:95
  82.4 2.0 copy-start.6
  82.4 2.1 copy-start.5
  86.0 2.9 copy-start.7
  91.3 160.0 %copy-start.8 = (f32[4608]{0:T(1024)S(1)}, f32[4608]{0:T(1024)}, u32[]{:S(2)}) copy-start(f32[4608]{0:T(1024)} %param.19) | copy-start | bytes 55300
  143.8 107.5 %all-gather.3.cloned.1.call-start = ((), (), s32[]{:S(2)}) async-start(), calls=%async_computation | async-start | bytes 5898240 | tf_op jit(solution)/shard_map/all_gather | solution.py:96
  144.6 238.7 %all-reduce.6.cloned.1.call-start = ((), (), s32[]{:S(2)}) async-start(), calls=%async_computation.2 | async-start | bytes 18874368 | tf_op jit(solution)/shard_map/psum | solution.py:110
  200.0 57.3 %copy-start.9 = (f32[4608]{0:T(1024)S(1)}, f32[4608]{0:T(1024)}, u32[]{:S(2)}) copy-start(f32[4608]{0:T(1024)} %param.23) | copy-start | bytes 55300
  200.0 57.3 %copy-start.12 = (f32[512]{0:T(512)S(1)}, f32[512]{0:T(512)}, u32[]{:S(2)}) copy-start(f32[512]{0:T(512)} %param.21) | copy-start | bytes 6148
  251.3 12.4 %slice-start = ((s8[4718592]{0:T(1024)(128)(4,1)}), s8[4194304]{0:T(1024)(128)(4,1)S(1)}, s32[]{:S(2)}) async-start(s8[4718592]{0:T(1024)(128)(4,1)} %bitcast.40), calls=%async_computation.5 | async-start | bytes 8388608
  257.3 6.4 %copy-start.2 = (bf16[512,4608]{1,0:T(8,128)(2,1)}, bf16[512,4608]{1,0:T(8,128)(2,1)S(1)}, u32[]{:S(2)}) copy-start(bf16[512,4608]{1,0:T(8,128)(2,1)S(1)} %fusion.3) | copy-start | bytes 14155780
  257.3 6.4 %slice-start.1 = ((s8[4718592]{0:T(1024)(128)(4,1)}), s8[524288]{0:T(1024)(128)(4,1)S(1)}, s32[]{:S(2)}) async-start(s8[4718592]{0:T(1024)(128)(4,1)} %bitcast.40), calls=%async_computation.6 | async-start | bytes 1048576
  268.8 268.4 %all-reduce.8.cloned.1.call-start = ((), (), s32[]{:S(2)}) async-start(), calls=%async_computation.3 | async-start | bytes 18874368 | tf_op jit(solution)/shard_map/psum | solution.py:110
  545.6 6.7 %copy-start.4 = (bf16[512,4608]{1,0:T(8,128)(2,1)}, bf16[512,4608]{1,0:T(8,128)(2,1)S(1)}, u32[]{:S(2)}) copy-start(bf16[512,4608]{1,0:T(8,128)(2,1)S(1)} %get-tuple-element.7) | copy-start | bytes 14155780
  559.7 7.9 %copy-start.1 = (bf16[512,1152]{1,0:T(8,128)(2,1)S(1)}, bf16[512,1152]{1,0:T(8,128)(2,1)}, u32[]{:S(2)}) copy-start(bf16[512,1152]{1,0:T(8,128)(2,1)} %param.18) | copy-start | bytes 3538948
Sparse Core Ops, SparseCore 0:
  15.1 61.7 all-reduce.9
  144.0 52.6 all-gather.4
  198.3 52.9 all-gather.2
  269.0 114.2 all-reduce.5
  386.8 150.4 all-reduce.7
